TPU v7x, 32 devices: a whole 2x2x4 slice. The times are simulated.
32 devices in a mesh: section: 4 (over x, core), obs: 8 (over z, y).
Axes of the slice: x: 2, y: 2, z: 4, core: 2. Of those that a mesh axis runs over, the one named last changes fastest.
Arguments:
- predictors: bfloat16 [4, 4, 20, 32768], P('section', None, None, 'obs'), may hold values from -5 to 5
- departures: float32 [4, 4, 32768], P('section', None, 'obs'), may hold values from -30 to 30
- obs_precision: float32 [4, 4, 32768], P('section', None, 'obs'), may hold values from 0.3 to 3
- qc_pass: int32 [4, 4, 32768], P('section', None, 'obs'), may hold values 0 or 1
- block_channel: int32 [4, 4, 256], P('section', None, 'obs'), may hold values from 0 to 2047, as said below
- stream_order: int32 [4], replicated, may hold values from 0 to 3, each once
- prior_coeffs: float32 [4, 20, 2048], P(None, None, 'obs'), may hold values from -1 to 1
- prior_info: float32 [4, 210, 2048], P(None, None, 'obs'), may hold values from -1 to 32, as said below
- memory_factor: float32 [2048], P('obs'), may hold values from 0.5 to 0.98
Outputs:
- coeffs: float32 [4, 4, 20, 2048], P('section', None, None, 'obs')
- information: float32 [4, 4, 210, 2048], P('section', None, None, 'obs')
Inputs may be any that keep to these rules, and one draw needn't show every extreme that they name: `block_channel`: among the 32 row blocks of one index of obs, at most 8 have channels in any one range of the 256 channels from a multiple of 256; in every window and stream one such range holds exactly 8 blocks of every index of obs. `stream_order`: each stream appears once. `prior_info`: for every stream and channel the 210 entries are the upper triangle, row by row, of a symmetric positive definite matrix of order 20.
All inputs are finite; a program needn't handle non-finite values. No bound on the sum of `qc_pass` on one device may be relied on, other than what follows from the above.
Results may differ from a plain program's by a relative error of at most 0.0038.
Values sent between devices are 32-bit elements; how exact they have to be, the bound alone decides.
A program may use at most 64 MiB of HBM per device.

v0:
```python
import jax
import jax.numpy as jnp
import numpy as np
from jax import lax
from jax.sharding import PartitionSpec as P

HUBER_SQ = 9.0
PRIOR_WEIGHT = 64.0


def from_behind(array, axis, by):
    size = lax.axis_size(axis)
    pairs = [(i, i + by) for i in range(size) if 0 <= i + by < size]
    return lax.ppermute(array, axis, pairs)


def upper_positions(dimension):
    return np.array(
        [i * dimension + j for i in range(dimension) for j in range(i, dimension)], dtype=np.int32
    )


def solve_packed(packed, target):
    dimension = target.shape[0]
    placing = {}
    counter = 0
    for i in range(dimension):
        for j in range(i, dimension):
            placing[i, j] = counter
            counter += 1
    factor = [[None] * dimension for i in range(dimension)]
    for j in range(dimension):
        pivot_root = jnp.sqrt(
            packed[placing[j, j]] - sum((factor[j][k] * factor[j][k] for k in range(j)))
        )
        factor[j][j] = pivot_root
        for i in range(j + 1, dimension):
            factor[i][j] = (
                packed[placing[j, i]] - sum((factor[i][k] * factor[j][k] for k in range(j)))
            ) / pivot_root
    forward = []
    for i in range(dimension):
        forward.append(
            (target[i] - sum((factor[i][k] * forward[k] for k in range(i)))) / factor[i][i]
        )
    backward = [None] * dimension
    for i in reversed(range(dimension)):
        backward[i] = (
            forward[i] - sum((factor[k][i] * backward[k] for k in range(i + 1, dimension)))
        ) / factor[i][i]
    return jnp.stack(backward)


def block_terms(predicted, departed, precision, passed, block_coeffs):
    pred_count, row_count = predicted.shape
    block_count = block_coeffs.shape[1]
    block_width = row_count // block_count
    upper_index = upper_positions(pred_count)
    shaped = predicted.reshape(pred_count, block_count, block_width)
    offset = jnp.sum(shaped.astype(jnp.float32) * block_coeffs[:, :, None], axis=0)
    residual = departed.reshape(block_count, block_width) - offset
    scale_row = precision.reshape(block_count, block_width)
    weight = (
        passed.reshape(block_count, block_width).astype(jnp.float32)
        * scale_row
        / (1.0 + scale_row * residual * residual / HUBER_SQ)
    )
    weighted = (weight[None] * shaped.astype(jnp.float32)).astype(jnp.bfloat16)
    chi_square = jnp.sum(weight * residual * residual)
    passed_count = jnp.sum(passed.astype(jnp.float32))
    gram_full = lax.dot_general(
        weighted, shaped, (((2,), (2,)), ((1,), (1,))), preferred_element_type=jnp.float32
    )
    gram_upper = gram_full.reshape(block_count, pred_count * pred_count)[:, upper_index]
    gradient = jnp.sum(weighted.astype(jnp.float32) * residual[None], axis=2).T
    return (jnp.concatenate([gram_upper, gradient], axis=1), jnp.stack([chi_square, passed_count]))


def local(
    predictors,
    departures,
    obs_precision,
    qc_pass,
    block_channel,
    stream_order,
    prior_coeffs,
    prior_info,
    memory_factor,
):
    section_count = lax.axis_size("section")
    obs_devices = lax.axis_size("obs")
    section_place = lax.axis_index("section")
    stream_count = stream_order.shape[0]
    local_channels = memory_factor.shape[0]
    block_count = block_channel.shape[2]
    pred_count = prior_coeffs.shape[1]
    tri_count = prior_info.shape[1]
    column_count = tri_count + pred_count
    capacity = 2 * block_count // obs_devices
    local_line = jnp.arange(local_channels, dtype=jnp.float32)
    owner_line = jnp.arange(obs_devices, dtype=jnp.int32)
    slot_line = jnp.arange(obs_devices * capacity, dtype=jnp.int32)
    highest = lax.Precision.HIGHEST

    def pack_blocks(block_sums, channel):
        owner_index = channel // local_channels
        inner_channel = channel % local_channels
        owner_hot = (owner_index[:, None] == owner_line[None, :]).astype(jnp.int32)
        ranking = jnp.sum((jnp.cumsum(owner_hot, axis=0) - 1) * owner_hot, axis=1)
        slot_of = owner_index * capacity + ranking
        placing = (slot_of[:, None] == slot_line[None, :]).astype(jnp.float32)
        send_rows = lax.dot_general(
            placing,
            block_sums,
            (((0,), (0,)), ((), ())),
            precision=highest,
            preferred_element_type=jnp.float32,
        ).reshape(obs_devices, capacity, column_count)
        send_channel = (
            lax.dot_general(
                placing,
                (inner_channel + 1).astype(jnp.float32),
                (((0,), (0,)), ((), ())),
                precision=highest,
                preferred_element_type=jnp.float32,
            ).reshape(obs_devices, capacity)
            - 1.0
        )
        return (send_rows, send_channel)

    def unpack_blocks(got_rows, got_channel):
        gather_hot = (got_channel.reshape(-1)[:, None] == local_line[None, :]).astype(jnp.float32)
        return lax.dot_general(
            got_rows.reshape(-1, column_count),
            gather_hot,
            (((0,), (0,)), ((), ())),
            precision=highest,
            preferred_element_type=jnp.float32,
        )

    def window_work(state_now, streams):
        beta_prior = state_now[:, :pred_count]
        info_prior = state_now[:, pred_count:]
        all_coeffs = lax.all_gather(beta_prior, "obs", axis=2, tiled=True)
        channel = jnp.take(block_channel[0], streams, axis=0)
        block_coeffs = jax.vmap(lambda coeff_rows, chan: jnp.take(coeff_rows, chan, axis=1))(
            all_coeffs, channel
        )
        block_sums, statistics = jax.vmap(block_terms)(
            jnp.take(predictors[0], streams, axis=0),
            jnp.take(departures[0], streams, axis=0),
            jnp.take(obs_precision[0], streams, axis=0),
            jnp.take(qc_pass[0], streams, axis=0),
            block_coeffs,
        )
        totals = lax.psum(statistics, "obs")
        send_rows, send_channel = jax.vmap(pack_blocks)(block_sums, channel)
        got_rows, got_channel = (
            lax.all_to_all(send_rows, "obs", split_axis=1, concat_axis=1, tiled=True),
            lax.all_to_all(send_channel, "obs", split_axis=1, concat_axis=1, tiled=True),
        )
        normal = jax.vmap(unpack_blocks)(got_rows, got_channel)
        inflation = (totals[:, 0] + PRIOR_WEIGHT) / (totals[:, 1] + PRIOR_WEIGHT)
        info_post = info_prior + normal[:, :tri_count] / inflation[:, None, None]
        beta_post = beta_prior + jax.vmap(solve_packed)(
            info_post, normal[:, tri_count:] / inflation[:, None, None]
        )
        outgoing = jnp.concatenate([beta_post, memory_factor[None, None, :] * info_post], axis=1)
        incoming = from_behind(outgoing, "section", 1)
        return (beta_post, info_post, incoming)

    def fresh_of(streams):
        return jnp.concatenate(
            [jnp.take(prior_coeffs, streams, axis=0), jnp.take(prior_info, streams, axis=0)], axis=1
        )

    coeff_start = jnp.zeros((1, stream_count, pred_count, local_channels), jnp.float32)
    info_start = jnp.zeros((1, stream_count, tri_count, local_channels), jnp.float32)

    def tick_step(t, loop_state):
        incoming, coeff_out, info_out = loop_state
        entry_index = t - section_place
        usable = (entry_index >= 0) & (entry_index < stream_count)
        slot_index = jnp.clip(entry_index, 0, stream_count - 1)
        streams = lax.dynamic_slice_in_dim(stream_order, slot_index, 1, 0)
        state_now = jnp.where(
            (section_place == 0) | jnp.logical_not(usable), fresh_of(streams), incoming
        )
        beta_post, info_post, incoming = window_work(state_now, streams)

        def store_entry(buffer, result):
            current = lax.dynamic_slice_in_dim(buffer, slot_index, 1, 1)
            updated = jnp.where(usable, result[None], current)
            return lax.dynamic_update_slice_in_dim(buffer, updated, slot_index, 1)

        return (incoming, store_entry(coeff_out, beta_post), store_entry(info_out, info_post))

    initial = (jnp.zeros((1, column_count, local_channels), jnp.float32), coeff_start, info_start)
    final_state = lax.fori_loop(0, stream_count + section_count - 1, tick_step, initial)
    return (final_state[1], final_state[2])


def solution(mesh):
    in_specs = (
        P("section", None, None, "obs"),
        P("section", None, "obs"),
        P("section", None, "obs"),
        P("section", None, "obs"),
        P("section", None, "obs"),
        P(),
        P(None, None, "obs"),
        P(None, None, "obs"),
        P("obs"),
    )
    out_specs = (P("section", None, None, "obs"), P("section", None, None, "obs"))
    return jax.shard_map(local, mesh=mesh, in_specs=in_specs, out_specs=out_specs, check_vma=False)
```

profile of v0, /device:TPU:1, one launch (start us, length us, event | category | flops | bytes accessed | tf_op | source)
XLA Modules:
  0.0 688.5 jit_solution(5905409147109336993)
XLA Ops:
  2.9 684.6 %while.38 = (s32[]{:T(128)}, f32[1,230,256]{2,1,0:T(8,128)S(1)}, f32[1,4,20,256]{3,1,2,0:T(4,128)S(1)}, f32[1,4,210,256]{3,1,2,0:T(4,128)S(1)}, s32[]{:T(128)}, ...) while((s32[]{:T(128)}, f32[1,230,256]{2,1,0:T(8,128)S(1)}, ...), condition=%wide.region_8.10_spmd.clone.clone, body=%wide.region_0.9_spmd.sunk.clone.clone.sunk | while | flops 57759508 | bytes 13853709 | solution.py:199
  7.5 6.4 all-to-all-start.1
  16.3 24.6 %all_gather.15 = f32[1,20,2048]{2,1,0:T(8,128)S(1)} all-gather(f32[1,20,256]{2,1,0:T(8,128)S(1)} %slice.5342), channel_id=1, replica_groups=mesh['section'=4,'obs'=8] {'obs'}, dimensions={2}, use_global_device_ids=true | all-gather | bytes 184320 | tf_op jit(solution)/shard_map/while/body/eval_jaxpr/all_gather | solution.py:144
  47.6 17.5 %psum.19 = f32[1,2]{1,0:T(1,128)S(1)} all-reduce(f32[1,2]{1,0:T(1,128)S(1)} %maximum_bitcast_fusion.6), channel_id=1, replica_groups=mesh['section'=4,'obs'=8] {'obs'}, use_global_device_ids=true, to_apply=%region_7.8 | all-reduce | flops 2 | bytes 16 | tf_op jit(solution)/shard_map/while/body/eval_jaxpr/psum | solution.py:156
  72.6 4.4 all-to-all-done
  83.2 15.7 %collective-permute-start = (f32[1,230,256]{2,1,0:T(8,128)S(1)}, f32[1,230,256]{2,1,0:T(8,128)S(1)}, u32[]{:S(2)}, u32[]{:S(2)}) collective-permute-start(f32[1,230,256]{2,1,0:T(8,128)S(1)} %pad_maximum_fusion.2), channel_id=1, source_target_pairs={{0,8},{8,16},{16,24},{1,9},{9,17},{17,25},{2,10},{10,18},{18,26},{... | collective-permute-start | bytes 706568 | tf_op jit(solution)/shard_map/while/body/eval_jaxpr/ppermute | solution.py:14
  99.3 5.9 dynamic_update_slice.31
  115.6 25.2 %all_gather.15 = f32[1,20,2048]{2,1,0:T(8,128)S(1)} all-gather(f32[1,20,256]{2,1,0:T(8,128)S(1)} %slice.5342), channel_id=1, replica_groups=mesh['section'=4,'obs'=8] {'obs'}, dimensions={2}, use_global_device_ids=true | all-gather | bytes 184320 | tf_op jit(solution)/shard_map/while/body/eval_jaxpr/all_gather | solution.py:144
  147.5 17.3 %psum.19 = f32[1,2]{1,0:T(1,128)S(1)} all-reduce(f32[1,2]{1,0:T(1,128)S(1)} %maximum_bitcast_fusion.6), channel_id=1, replica_groups=mesh['section'=4,'obs'=8] {'obs'}, use_global_device_ids=true, to_apply=%region_7.8 | all-reduce | flops 2 | bytes 16 | tf_op jit(solution)/shard_map/while/body/eval_jaxpr/psum | solution.py:156
  172.3 4.4 all-to-all-done
  182.9 13.1 %collective-permute-start = (f32[1,230,256]{2,1,0:T(8,128)S(1)}, f32[1,230,256]{2,1,0:T(8,128)S(1)}, u32[]{:S(2)}, u32[]{:S(2)}) collective-permute-start(f32[1,230,256]{2,1,0:T(8,128)S(1)} %pad_maximum_fusion.2), channel_id=1, source_target_pairs={{0,8},{8,16},{16,24},{1,9},{9,17},{17,25},{2,10},{10,18},{18,26},{... | collective-permute-start | bytes 706568 | tf_op jit(solution)/shard_map/while/body/eval_jaxpr/ppermute | solution.py:14
  196.4 5.9 dynamic_update_slice.31
  212.6 24.6 %all_gather.15 = f32[1,20,2048]{2,1,0:T(8,128)S(1)} all-gather(f32[1,20,256]{2,1,0:T(8,128)S(1)} %slice.5342), channel_id=1, replica_groups=mesh['section'=4,'obs'=8] {'obs'}, dimensions={2}, use_global_device_ids=true | all-gather | bytes 184320 | tf_op jit(solution)/shard_map/while/body/eval_jaxpr/all_gather | solution.py:144
  244.0 17.5 %psum.19 = f32[1,2]{1,0:T(1,128)S(1)} all-reduce(f32[1,2]{1,0:T(1,128)S(1)} %maximum_bitcast_fusion.6), channel_id=1, replica_groups=mesh['section'=4,'obs'=8] {'obs'}, use_global_device_ids=true, to_apply=%region_7.8 | all-reduce | flops 2 | bytes 16 | tf_op jit(solution)/shard_map/while/body/eval_jaxpr/psum | solution.py:156
  279.6 13.4 %collective-permute-start = (f32[1,230,256]{2,1,0:T(8,128)S(1)}, f32[1,230,256]{2,1,0:T(8,128)S(1)}, u32[]{:S(2)}, u32[]{:S(2)}) collective-permute-start(f32[1,230,256]{2,1,0:T(8,128)S(1)} %pad_maximum_fusion.2), channel_id=1, source_target_pairs={{0,8},{8,16},{16,24},{1,9},{9,17},{17,25},{2,10},{10,18},{18,26},{... | collective-permute-start | bytes 706568 | tf_op jit(solution)/shard_map/while/body/eval_jaxpr/ppermute | solution.py:14
  293.4 5.9 dynamic_update_slice.31
  309.7 24.8 %all_gather.15 = f32[1,20,2048]{2,1,0:T(8,128)S(1)} all-gather(f32[1,20,256]{2,1,0:T(8,128)S(1)} %slice.5342), channel_id=1, replica_groups=mesh['section'=4,'obs'=8] {'obs'}, dimensions={2}, use_global_device_ids=true | all-gather | bytes 184320 | tf_op jit(solution)/shard_map/while/body/eval_jaxpr/all_gather | solution.py:144
  341.3 17.6 %psum.19 = f32[1,2]{1,0:T(1,128)S(1)} all-reduce(f32[1,2]{1,0:T(1,128)S(1)} %maximum_bitcast_fusion.6), channel_id=1, replica_groups=mesh['section'=4,'obs'=8] {'obs'}, use_global_device_ids=true, to_apply=%region_7.8 | all-reduce | flops 2 | bytes 16 | tf_op jit(solution)/shard_map/while/body/eval_jaxpr/psum | solution.py:156
  377.0 13.1 %collective-permute-start = (f32[1,230,256]{2,1,0:T(8,128)S(1)}, f32[1,230,256]{2,1,0:T(8,128)S(1)}, u32[]{:S(2)}, u32[]{:S(2)}) collective-permute-start(f32[1,230,256]{2,1,0:T(8,128)S(1)} %pad_maximum_fusion.2), channel_id=1, source_target_pairs={{0,8},{8,16},{16,24},{1,9},{9,17},{17,25},{2,10},{10,18},{18,26},{... | collective-permute-start | bytes 706568 | tf_op jit(solution)/shard_map/while/body/eval_jaxpr/ppermute | solution.py:14
  390.5 5.9 dynamic_update_slice.31
  406.7 24.9 %all_gather.15 = f32[1,20,2048]{2,1,0:T(8,128)S(1)} all-gather(f32[1,20,256]{2,1,0:T(8,128)S(1)} %slice.5342), channel_id=1, replica_groups=mesh['section'=4,'obs'=8] {'obs'}, dimensions={2}, use_global_device_ids=true | all-gather | bytes 184320 | tf_op jit(solution)/shard_map/while/body/eval_jaxpr/all_gather | solution.py:144
  438.4 17.2 %psum.19 = f32[1,2]{1,0:T(1,128)S(1)} all-reduce(f32[1,2]{1,0:T(1,128)S(1)} %maximum_bitcast_fusion.6), channel_id=1, replica_groups=mesh['section'=4,'obs'=8] {'obs'}, use_global_device_ids=true, to_apply=%region_7.8 | all-reduce | flops 2 | bytes 16 | tf_op jit(solution)/shard_map/while/body/eval_jaxpr/psum | solution.py:156
  473.8 13.4 %collective-permute-start = (f32[1,230,256]{2,1,0:T(8,128)S(1)}, f32[1,230,256]{2,1,0:T(8,128)S(1)}, u32[]{:S(2)}, u32[]{:S(2)}) collective-permute-start(f32[1,230,256]{2,1,0:T(8,128)S(1)} %pad_maximum_fusion.2), channel_id=1, source_target_pairs={{0,8},{8,16},{16,24},{1,9},{9,17},{17,25},{2,10},{10,18},{18,26},{... | collective-permute-start | bytes 706568 | tf_op jit(solution)/shard_map/while/body/eval_jaxpr/ppermute | solution.py:14
  487.5 5.9 dynamic_update_slice.31
  503.8 24.8 %all_gather.15 = f32[1,20,2048]{2,1,0:T(8,128)S(1)} all-gather(f32[1,20,256]{2,1,0:T(8,128)S(1)} %slice.5342), channel_id=1, replica_groups=mesh['section'=4,'obs'=8] {'obs'}, dimensions={2}, use_global_device_ids=true | all-gather | bytes 184320 | tf_op jit(solution)/shard_map/while/body/eval_jaxpr/all_gather | solution.py:144
  535.4 17.5 %psum.19 = f32[1,2]{1,0:T(1,128)S(1)} all-reduce(f32[1,2]{1,0:T(1,128)S(1)} %maximum_bitcast_fusion.6), channel_id=1, replica_groups=mesh['section'=4,'obs'=8] {'obs'}, use_global_device_ids=true, to_apply=%region_7.8 | all-reduce | flops 2 | bytes 16 | tf_op jit(solution)/shard_map/while/body/eval_jaxpr/psum | solution.py:156
  571.0 13.2 %collective-permute-start = (f32[1,230,256]{2,1,0:T(8,128)S(1)}, f32[1,230,256]{2,1,0:T(8,128)S(1)}, u32[]{:S(2)}, u32[]{:S(2)}) collective-permute-start(f32[1,230,256]{2,1,0:T(8,128)S(1)} %pad_maximum_fusion.2), channel_id=1, source_target_pairs={{0,8},{8,16},{16,24},{1,9},{9,17},{17,25},{2,10},{10,18},{18,26},{... | collective-permute-start | bytes 706568 | tf_op jit(solution)/shard_map/while/body/eval_jaxpr/ppermute | solution.py:14
  584.6 5.9 dynamic_update_slice.31
  600.9 24.5 %all_gather.15 = f32[1,20,2048]{2,1,0:T(8,128)S(1)} all-gather(f32[1,20,256]{2,1,0:T(8,128)S(1)} %slice.5342), channel_id=1, replica_groups=mesh['section'=4,'obs'=8] {'obs'}, dimensions={2}, use_global_device_ids=true | all-gather | bytes 184320 | tf_op jit(solution)/shard_map/while/body/eval_jaxpr/all_gather | solution.py:144
  632.1 18.0 %psum.19 = f32[1,2]{1,0:T(1,128)S(1)} all-reduce(f32[1,2]{1,0:T(1,128)S(1)} %maximum_bitcast_fusion.6), channel_id=1, replica_groups=mesh['section'=4,'obs'=8] {'obs'}, use_global_device_ids=true, to_apply=%region_7.8 | all-reduce | flops 2 | bytes 16 | tf_op jit(solution)/shard_map/while/body/eval_jaxpr/psum | solution.py:156
  668.2 13.1 %collective-permute-start = (f32[1,230,256]{2,1,0:T(8,128)S(1)}, f32[1,230,256]{2,1,0:T(8,128)S(1)}, u32[]{:S(2)}, u32[]{:S(2)}) collective-permute-start(f32[1,230,256]{2,1,0:T(8,128)S(1)} %pad_maximum_fusion.2), channel_id=1, source_target_pairs={{0,8},{8,16},{16,24},{1,9},{9,17},{17,25},{2,10},{10,18},{18,26},{... | collective-permute-start | bytes 706568 | tf_op jit(solution)/shard_map/while/body/eval_jaxpr/ppermute | solution.py:14
  681.7 5.9 dynamic_update_slice.31
  (648 shorter events, 214.5 us)
Async XLA Ops:
  2.2 0.7 copy-start.4
  2.3 0.7 copy-start.5
  7.5 60.4 %all-to-all-start.1 = ((f32[1,8,8]{2,0,1:T(1,128)}), f32[1,8,8]{2,0,1:T(1,128)S(1)}, u32[]{:S(2)}, u32[]{:S(2)}) async-start(f32[1,8,8]{2,0,1:T(1,128)} %bitcast.2454), calls=%async_computation.1 | async-start | bytes 8192 | tf_op jit(solution)/shard_map/while/body/eval_jaxpr/all_to_all | solution.py:160
  68.0 9.1 %all-to-all-start = ((f32[1,8,8,230]{3,2,0,1:T(8,128)}), f32[1,8,8,230]{3,2,0,1:T(8,128)S(1)}, u32[]{:S(2)}, u32[]{:S(2)}) async-start(f32[1,8,8,230]{3,2,0,1:T(8,128)} %convolution_bitcast_fusion.4), calls=%async_computation | async-start | bytes 131072 | tf_op jit(solution)/shard_map/while/body/eval_jaxpr/all_to_all | solution.py:159
  80.7 0.7 copy-start.1
  83.2 22.0 %collective-permute-start = (f32[1,230,256]{2,1,0:T(8,128)S(1)}, f32[1,230,256]{2,1,0:T(8,128)S(1)}, u32[]{:S(2)}, u32[]{:S(2)}) collective-permute-start(f32[1,230,256]{2,1,0:T(8,128)S(1)} %pad_maximum_fusion.2), channel_id=1, source_target_pairs={{0,8},{8,16},{16,24},{1,9},{9,17},{17,25},{2,10},{10,18},{18,26},{... | collective-permute-start | bytes 706568 | tf_op jit(solution)/shard_map/while/body/eval_jaxpr/ppermute | solution.py:14
  109.8 57.8 %all-to-all-start.1 = ((f32[1,8,8]{2,0,1:T(1,128)}), f32[1,8,8]{2,0,1:T(1,128)S(1)}, u32[]{:S(2)}, u32[]{:S(2)}) async-start(f32[1,8,8]{2,0,1:T(1,128)} %bitcast.2454), calls=%async_computation.1 | async-start | bytes 8192 | tf_op jit(solution)/shard_map/while/body/eval_jaxpr/all_to_all | solution.py:160
  167.6 9.1 %all-to-all-start = ((f32[1,8,8,230]{3,2,0,1:T(8,128)}), f32[1,8,8,230]{3,2,0,1:T(8,128)S(1)}, u32[]{:S(2)}, u32[]{:S(2)}) async-start(f32[1,8,8,230]{3,2,0,1:T(8,128)} %convolution_bitcast_fusion.4), calls=%async_computation | async-start | bytes 131072 | tf_op jit(solution)/shard_map/while/body/eval_jaxpr/all_to_all | solution.py:159
  180.4 0.7 copy-start.1
  182.9 19.4 %collective-permute-start = (f32[1,230,256]{2,1,0:T(8,128)S(1)}, f32[1,230,256]{2,1,0:T(8,128)S(1)}, u32[]{:S(2)}, u32[]{:S(2)}) collective-permute-start(f32[1,230,256]{2,1,0:T(8,128)S(1)} %pad_maximum_fusion.2), channel_id=1, source_target_pairs={{0,8},{8,16},{16,24},{1,9},{9,17},{17,25},{2,10},{10,18},{18,26},{... | collective-permute-start | bytes 706568 | tf_op jit(solution)/shard_map/while/body/eval_jaxpr/ppermute | solution.py:14
  206.9 57.5 %all-to-all-start.1 = ((f32[1,8,8]{2,0,1:T(1,128)}), f32[1,8,8]{2,0,1:T(1,128)S(1)}, u32[]{:S(2)}, u32[]{:S(2)}) async-start(f32[1,8,8]{2,0,1:T(1,128)} %bitcast.2454), calls=%async_computation.1 | async-start | bytes 8192 | tf_op jit(solution)/shard_map/while/body/eval_jaxpr/all_to_all | solution.py:160
  264.4 9.1 %all-to-all-start = ((f32[1,8,8,230]{3,2,0,1:T(8,128)}), f32[1,8,8,230]{3,2,0,1:T(8,128)S(1)}, u32[]{:S(2)}, u32[]{:S(2)}) async-start(f32[1,8,8,230]{3,2,0,1:T(8,128)} %convolution_bitcast_fusion.4), calls=%async_computation | async-start | bytes 131072 | tf_op jit(solution)/shard_map/while/body/eval_jaxpr/all_to_all | solution.py:159
  277.1 0.7 copy-start.1
  279.6 19.7 %collective-permute-start = (f32[1,230,256]{2,1,0:T(8,128)S(1)}, f32[1,230,256]{2,1,0:T(8,128)S(1)}, u32[]{:S(2)}, u32[]{:S(2)}) collective-permute-start(f32[1,230,256]{2,1,0:T(8,128)S(1)} %pad_maximum_fusion.2), channel_id=1, source_target_pairs={{0,8},{8,16},{16,24},{1,9},{9,17},{17,25},{2,10},{10,18},{18,26},{... | collective-permute-start | bytes 706568 | tf_op jit(solution)/shard_map/while/body/eval_jaxpr/ppermute | solution.py:14
  303.9 57.8 %all-to-all-start.1 = ((f32[1,8,8]{2,0,1:T(1,128)}), f32[1,8,8]{2,0,1:T(1,128)S(1)}, u32[]{:S(2)}, u32[]{:S(2)}) async-start(f32[1,8,8]{2,0,1:T(1,128)} %bitcast.2454), calls=%async_computation.1 | async-start | bytes 8192 | tf_op jit(solution)/shard_map/while/body/eval_jaxpr/all_to_all | solution.py:160
  361.8 9.1 %all-to-all-start = ((f32[1,8,8,230]{3,2,0,1:T(8,128)}), f32[1,8,8,230]{3,2,0,1:T(8,128)S(1)}, u32[]{:S(2)}, u32[]{:S(2)}) async-start(f32[1,8,8,230]{3,2,0,1:T(8,128)} %convolution_bitcast_fusion.4), calls=%async_computation | async-start | bytes 131072 | tf_op jit(solution)/shard_map/while/body/eval_jaxpr/all_to_all | solution.py:159
  374.5 0.7 copy-start.1
  377.0 19.4 %collective-permute-start = (f32[1,230,256]{2,1,0:T(8,128)S(1)}, f32[1,230,256]{2,1,0:T(8,128)S(1)}, u32[]{:S(2)}, u32[]{:S(2)}) collective-permute-start(f32[1,230,256]{2,1,0:T(8,128)S(1)} %pad_maximum_fusion.2), channel_id=1, source_target_pairs={{0,8},{8,16},{16,24},{1,9},{9,17},{17,25},{2,10},{10,18},{18,26},{... | collective-permute-start | bytes 706568 | tf_op jit(solution)/shard_map/while/body/eval_jaxpr/ppermute | solution.py:14
  401.0 57.5 %all-to-all-start.1 = ((f32[1,8,8]{2,0,1:T(1,128)}), f32[1,8,8]{2,0,1:T(1,128)S(1)}, u32[]{:S(2)}, u32[]{:S(2)}) async-start(f32[1,8,8]{2,0,1:T(1,128)} %bitcast.2454), calls=%async_computation.1 | async-start | bytes 8192 | tf_op jit(solution)/shard_map/while/body/eval_jaxpr/all_to_all | solution.py:160
  458.5 9.1 %all-to-all-start = ((f32[1,8,8,230]{3,2,0,1:T(8,128)}), f32[1,8,8,230]{3,2,0,1:T(8,128)S(1)}, u32[]{:S(2)}, u32[]{:S(2)}) async-start(f32[1,8,8,230]{3,2,0,1:T(8,128)} %convolution_bitcast_fusion.4), calls=%async_computation | async-start | bytes 131072 | tf_op jit(solution)/shard_map/while/body/eval_jaxpr/all_to_all | solution.py:159
  471.3 0.7 copy-start.1
  473.8 19.7 %collective-permute-start = (f32[1,230,256]{2,1,0:T(8,128)S(1)}, f32[1,230,256]{2,1,0:T(8,128)S(1)}, u32[]{:S(2)}, u32[]{:S(2)}) collective-permute-start(f32[1,230,256]{2,1,0:T(8,128)S(1)} %pad_maximum_fusion.2), channel_id=1, source_target_pairs={{0,8},{8,16},{16,24},{1,9},{9,17},{17,25},{2,10},{10,18},{18,26},{... | collective-permute-start | bytes 706568 | tf_op jit(solution)/shard_map/while/body/eval_jaxpr/ppermute | solution.py:14
  498.1 57.7 %all-to-all-start.1 = ((f32[1,8,8]{2,0,1:T(1,128)}), f32[1,8,8]{2,0,1:T(1,128)S(1)}, u32[]{:S(2)}, u32[]{:S(2)}) async-start(f32[1,8,8]{2,0,1:T(1,128)} %bitcast.2454), calls=%async_computation.1 | async-start | bytes 8192 | tf_op jit(solution)/shard_map/while/body/eval_jaxpr/all_to_all | solution.py:160
  555.8 9.1 %all-to-all-start = ((f32[1,8,8,230]{3,2,0,1:T(8,128)}), f32[1,8,8,230]{3,2,0,1:T(8,128)S(1)}, u32[]{:S(2)}, u32[]{:S(2)}) async-start(f32[1,8,8,230]{3,2,0,1:T(8,128)} %convolution_bitcast_fusion.4), calls=%async_computation | async-start | bytes 131072 | tf_op jit(solution)/shard_map/while/body/eval_jaxpr/all_to_all | solution.py:159
  568.5 0.7 copy-start.1
  571.0 19.5 %collective-permute-start = (f32[1,230,256]{2,1,0:T(8,128)S(1)}, f32[1,230,256]{2,1,0:T(8,128)S(1)}, u32[]{:S(2)}, u32[]{:S(2)}) collective-permute-start(f32[1,230,256]{2,1,0:T(8,128)S(1)} %pad_maximum_fusion.2), channel_id=1, source_target_pairs={{0,8},{8,16},{16,24},{1,9},{9,17},{17,25},{2,10},{10,18},{18,26},{... | collective-permute-start | bytes 706568 | tf_op jit(solution)/shard_map/while/body/eval_jaxpr/ppermute | solution.py:14
  595.1 57.8 %all-to-all-start.1 = ((f32[1,8,8]{2,0,1:T(1,128)}), f32[1,8,8]{2,0,1:T(1,128)S(1)}, u32[]{:S(2)}, u32[]{:S(2)}) async-start(f32[1,8,8]{2,0,1:T(1,128)} %bitcast.2454), calls=%async_computation.1 | async-start | bytes 8192 | tf_op jit(solution)/shard_map/while/body/eval_jaxpr/all_to_all | solution.py:160
  652.9 9.1 %all-to-all-start = ((f32[1,8,8,230]{3,2,0,1:T(8,128)}), f32[1,8,8,230]{3,2,0,1:T(8,128)S(1)}, u32[]{:S(2)}, u32[]{:S(2)}) async-start(f32[1,8,8,230]{3,2,0,1:T(8,128)} %convolution_bitcast_fusion.4), calls=%async_computation | async-start | bytes 131072 | tf_op jit(solution)/shard_map/while/body/eval_jaxpr/all_to_all | solution.py:159
  665.7 0.7 copy-start.1
  668.2 19.4 %collective-permute-start = (f32[1,230,256]{2,1,0:T(8,128)S(1)}, f32[1,230,256]{2,1,0:T(8,128)S(1)}, u32[]{:S(2)}, u32[]{:S(2)}) collective-permute-start(f32[1,230,256]{2,1,0:T(8,128)S(1)} %pad_maximum_fusion.2), channel_id=1, source_target_pairs={{0,8},{8,16},{16,24},{1,9},{9,17},{17,25},{2,10},{10,18},{18,26},{... | collective-permute-start | bytes 706568 | tf_op jit(solution)/shard_map/while/body/eval_jaxpr/ppermute | solution.py:14
  687.6 0.9 copy-start.2
  687.6 0.9 copy-start.3
  (15 other events, 9.7 us)
where the time goes:
time: 692 us; the launch traced here: 689 us
  blocking collectives  296 us (43%)
  starting transfers between devices  145 us (21%)
  local copies, waits for them, and re-layouts  109 us (16%)
  other arithmetic  68.2 us (10%)
  waiting for transfers between devices  30.8 us (4%)
  loops' own time  25.7 us (4%)
  matrix products  12.9 us (2%)
    all_gather x7, blocking collectives, window_work(): all_coeffs = lax.all_gather(beta_prior, 'obs', axis=2, tiled=True)  173 us
    psum x7, blocking collectives, window_work(): totals = lax.psum(statistics, 'obs')  123 us
    ppermute x7, starting transfers between devices, from_behind(): return lax.ppermute(array, axis, pairs)  95 us
    dynamic_update_slice x28, local copies, waits for them, and re-layouts, store_entry(): return lax.dynamic_update_slice_in_dim(buffer, updated, slot_index, 1)  43.8 us
    all_to_all x7, waiting for transfers between devices, window_work(): lax.all_to_all(send_rows, 'obs', split_axis=1, concat_axis=1, tiled=True)  30.8 us
    all_to_all x7, starting transfers between devices, window_work(): lax.all_to_all(send_channel, 'obs', split_axis=1, concat_axis=1, tiled=True)  26.2 us
    another operation x1, loops' own time, local(): lax.fori_loop(0, stream_count + section_count - 1, tick_step, initial)  25.7 us
    all_to_all x7, starting transfers between devices, window_work(): lax.all_to_all(send_rows, 'obs', split_axis=1, concat_axis=1, tiled=True)  23.5 us
  transfers between devices with their start and end apart: 21, of which 7 were waited for; matrix products, arithmetic and copies ran while one was open for 18% of the time, Pallas kernels for 0%

commit v1 on v0

--- a/solution.py
+++ b/solution.py
@@ -153,7 +153,9 @@
             jnp.take(qc_pass[0], streams, axis=0),
             block_coeffs,
         )
-        totals = lax.psum(statistics, "obs")
+        totals = statistics
+        for hop in (1, 2, 4):
+            totals = totals + lax.ppermute(totals, "obs", [(dev, dev ^ hop) for dev in range(8)])
         send_rows, send_channel = jax.vmap(pack_blocks)(block_sums, channel)
         got_rows, got_channel = (
             lax.all_to_all(send_rows, "obs", split_axis=1, concat_axis=1, tiled=True),

time: 692 us -> 626 us (0.905)
  blocking collectives: 296 us -> 174 us
  starting transfers between devices: 145 us -> 167 us
  other arithmetic: 68.2 us -> 86.9 us
  waiting for transfers between devices: 30.8 us -> 46.8 us
    psum x7 -> x0, blocking collectives: 123 us -> none  [window_work(): totals = lax.psum(statistics, 'obs')]
    ppermute x0 -> x21, waiting for transfers between devices: none -> 27.8 us  [window_work(): lax.ppermute(totals, 'obs', [(dev, dev ^ hop) for dev in range(8)])]
    ppermute x0 -> x21, starting transfers between devices: none -> 21 us  [window_work(): lax.ppermute(totals, 'obs', [(dev, dev ^ hop) for dev in range(8)])]
    add x0 -> x21, other arithmetic: none -> 18.5 us  [window_work(): totals + lax.ppermute(totals, 'obs', [(dev, dev ^ hop) for dev in range(8)])]
    all_to_all x7, waiting for transfers between devices: 30.8 us -> 19 us  [window_work(): lax.all_to_all(send_rows, 'obs', split_axis=1, concat_axis=1, tiled=True)]
  transfers between devices with their start and end apart: 21 -> 42, of which waited for: 7 -> 21; matrix products, arithmetic and copies ran while one was open for 18% -> 23% of each run, Pallas kernels for 0% -> 0%
where the time goes in v1:
time: 626 us; the launch traced here: 623 us
  blocking collectives  174 us (28%)
  starting transfers between devices  167 us (27%)
  local copies, waits for them, and re-layouts  109 us (17%)
  other arithmetic  86.9 us (14%)
  waiting for transfers between devices  46.8 us (7%)
  loops' own time  26 us (4%)
  matrix products  12.9 us (2%)
    all_gather x7, blocking collectives, window_work(): all_coeffs = lax.all_gather(beta_prior, 'obs', axis=2, tiled=True)  174 us
    ppermute x7, starting transfers between devices, from_behind(): return lax.ppermute(array, axis, pairs)  89.8 us
    dynamic_update_slice x28, local copies, waits for them, and re-layouts, store_entry(): return lax.dynamic_update_slice_in_dim(buffer, updated, slot_index, 1)  43.8 us
    all_to_all x7, starting transfers between devices, window_work(): lax.all_to_all(send_rows, 'obs', split_axis=1, concat_axis=1, tiled=True)  29.5 us
    ppermute x21, waiting for transfers between devices, window_work(): lax.ppermute(totals, 'obs', [(dev, dev ^ hop) for dev in range(8)])  27.8 us
    all_to_all x7, starting transfers between devices, window_work(): lax.all_to_all(send_channel, 'obs', split_axis=1, concat_axis=1, tiled=True)  26.2 us
    another operation x1, loops' own time, local(): lax.fori_loop(0, stream_count + section_count - 1, tick_step, initial)  26 us
    ppermute x21, starting transfers between devices, window_work(): lax.ppermute(totals, 'obs', [(dev, dev ^ hop) for dev in range(8)])  21 us
  transfers between devices with their start and end apart: 42, of which 21 were waited for; matrix products, arithmetic and copies ran while one was open for 23% of the time, Pallas kernels for 0%

profile of v1, /device:TPU:1, one launch (start us, length us, event | category | flops | bytes accessed | tf_op | source)
XLA Modules:
  0.0 622.7 jit_solution(4866859668930999702)
XLA Ops:
  2.9 618.9 %while.38 = (s32[]{:T(128)}, f32[1,230,256]{2,1,0:T(8,128)S(1)}, f32[1,4,20,256]{3,1,2,0:T(4,128)S(1)}, f32[1,4,210,256]{3,1,2,0:T(4,128)S(1)}, s32[]{:T(128)}, ...) while((s32[]{:T(128)}, f32[1,230,256]{2,1,0:T(8,128)S(1)}, ...), condition=%wide.region_7.9_spmd.clone.clone, body=%wide.region_0.8_spmd.sunk.clone.clone.sunk | while | flops 57759520 | bytes 13853989 | solution.py:201
  7.5 6.4 %all-to-all-start.1 = ((f32[1,8,8]{2,0,1:T(1,128)}), f32[1,8,8]{2,0,1:T(1,128)S(1)}, u32[]{:S(2)}, u32[]{:S(2)}) async-start(f32[1,8,8]{2,0,1:T(1,128)} %bitcast.2462), calls=%async_computation.1 | async-start | bytes 8192 | tf_op jit(solution)/shard_map/while/body/eval_jaxpr/all_to_all | solution.py:162
  16.3 24.6 %all_gather.15 = f32[1,20,2048]{2,1,0:T(8,128)S(1)} all-gather(f32[1,20,256]{2,1,0:T(8,128)S(1)} %slice.5342), channel_id=1, replica_groups=mesh['section'=4,'obs'=8] {'obs'}, dimensions={2}, use_global_device_ids=true | all-gather | bytes 184320 | tf_op jit(solution)/shard_map/while/body/eval_jaxpr/all_gather | solution.py:144
  58.3 4.3 all-to-all-start
  74.5 14.9 %collective-permute-start.3 = (f32[1,230,256]{2,1,0:T(8,128)S(1)}, f32[1,230,256]{2,1,0:T(8,128)S(1)}, u32[]{:S(2)}, u32[]{:S(2)}) collective-permute-start(f32[1,230,256]{2,1,0:T(8,128)S(1)} %pad_maximum_fusion.2), channel_id=1, source_target_pairs={{0,8},{8,16},{16,24},{1,9},{9,17},{17,25},{2,10},{10,18},{18,26},{... | collective-permute-start | bytes 706568 | tf_op jit(solution)/shard_map/while/body/eval_jaxpr/ppermute | solution.py:14
  89.8 5.9 dynamic_update_slice.31
  100.3 3.3 all-to-all-start.1
  106.1 25.2 %all_gather.15 = f32[1,20,2048]{2,1,0:T(8,128)S(1)} all-gather(f32[1,20,256]{2,1,0:T(8,128)S(1)} %slice.5342), channel_id=1, replica_groups=mesh['section'=4,'obs'=8] {'obs'}, dimensions={2}, use_global_device_ids=true | all-gather | bytes 184320 | tf_op jit(solution)/shard_map/while/body/eval_jaxpr/all_gather | solution.py:144
  148.4 4.3 all-to-all-start
  164.6 12.5 %collective-permute-start.3 = (f32[1,230,256]{2,1,0:T(8,128)S(1)}, f32[1,230,256]{2,1,0:T(8,128)S(1)}, u32[]{:S(2)}, u32[]{:S(2)}) collective-permute-start(f32[1,230,256]{2,1,0:T(8,128)S(1)} %pad_maximum_fusion.2), channel_id=1, source_target_pairs={{0,8},{8,16},{16,24},{1,9},{9,17},{17,25},{2,10},{10,18},{18,26},{... | collective-permute-start | bytes 706568 | tf_op jit(solution)/shard_map/while/body/eval_jaxpr/ppermute | solution.py:14
  177.5 5.9 dynamic_update_slice.31
  188.0 3.3 all-to-all-start.1
  193.8 24.8 %all_gather.15 = f32[1,20,2048]{2,1,0:T(8,128)S(1)} all-gather(f32[1,20,256]{2,1,0:T(8,128)S(1)} %slice.5342), channel_id=1, replica_groups=mesh['section'=4,'obs'=8] {'obs'}, dimensions={2}, use_global_device_ids=true | all-gather | bytes 184320 | tf_op jit(solution)/shard_map/while/body/eval_jaxpr/all_gather | solution.py:144
  236.0 4.3 all-to-all-start
  252.2 12.6 %collective-permute-start.3 = (f32[1,230,256]{2,1,0:T(8,128)S(1)}, f32[1,230,256]{2,1,0:T(8,128)S(1)}, u32[]{:S(2)}, u32[]{:S(2)}) collective-permute-start(f32[1,230,256]{2,1,0:T(8,128)S(1)} %pad_maximum_fusion.2), channel_id=1, source_target_pairs={{0,8},{8,16},{16,24},{1,9},{9,17},{17,25},{2,10},{10,18},{18,26},{... | collective-permute-start | bytes 706568 | tf_op jit(solution)/shard_map/while/body/eval_jaxpr/ppermute | solution.py:14
  265.2 5.9 dynamic_update_slice.31
  281.4 24.8 %all_gather.15 = f32[1,20,2048]{2,1,0:T(8,128)S(1)} all-gather(f32[1,20,256]{2,1,0:T(8,128)S(1)} %slice.5342), channel_id=1, replica_groups=mesh['section'=4,'obs'=8] {'obs'}, dimensions={2}, use_global_device_ids=true | all-gather | bytes 184320 | tf_op jit(solution)/shard_map/while/body/eval_jaxpr/all_gather | solution.py:144
  323.9 4.3 all-to-all-start
  340.1 12.4 %collective-permute-start.3 = (f32[1,230,256]{2,1,0:T(8,128)S(1)}, f32[1,230,256]{2,1,0:T(8,128)S(1)}, u32[]{:S(2)}, u32[]{:S(2)}) collective-permute-start(f32[1,230,256]{2,1,0:T(8,128)S(1)} %pad_maximum_fusion.2), channel_id=1, source_target_pairs={{0,8},{8,16},{16,24},{1,9},{9,17},{17,25},{2,10},{10,18},{18,26},{... | collective-permute-start | bytes 706568 | tf_op jit(solution)/shard_map/while/body/eval_jaxpr/ppermute | solution.py:14
  352.9 5.9 dynamic_update_slice.31
  369.1 24.9 %all_gather.15 = f32[1,20,2048]{2,1,0:T(8,128)S(1)} all-gather(f32[1,20,256]{2,1,0:T(8,128)S(1)} %slice.5342), channel_id=1, replica_groups=mesh['section'=4,'obs'=8] {'obs'}, dimensions={2}, use_global_device_ids=true | all-gather | bytes 184320 | tf_op jit(solution)/shard_map/while/body/eval_jaxpr/all_gather | solution.py:144
  411.6 4.0 all-to-all-start
  427.5 12.7 %collective-permute-start.3 = (f32[1,230,256]{2,1,0:T(8,128)S(1)}, f32[1,230,256]{2,1,0:T(8,128)S(1)}, u32[]{:S(2)}, u32[]{:S(2)}) collective-permute-start(f32[1,230,256]{2,1,0:T(8,128)S(1)} %pad_maximum_fusion.2), channel_id=1, source_target_pairs={{0,8},{8,16},{16,24},{1,9},{9,17},{17,25},{2,10},{10,18},{18,26},{... | collective-permute-start | bytes 706568 | tf_op jit(solution)/shard_map/while/body/eval_jaxpr/ppermute | solution.py:14
  440.5 5.9 dynamic_update_slice.31
  456.8 24.8 %all_gather.15 = f32[1,20,2048]{2,1,0:T(8,128)S(1)} all-gather(f32[1,20,256]{2,1,0:T(8,128)S(1)} %slice.5342), channel_id=1, replica_groups=mesh['section'=4,'obs'=8] {'obs'}, dimensions={2}, use_global_device_ids=true | all-gather | bytes 184320 | tf_op jit(solution)/shard_map/while/body/eval_jaxpr/all_gather | solution.py:144
  499.1 4.3 all-to-all-start
  515.3 12.5 %collective-permute-start.3 = (f32[1,230,256]{2,1,0:T(8,128)S(1)}, f32[1,230,256]{2,1,0:T(8,128)S(1)}, u32[]{:S(2)}, u32[]{:S(2)}) collective-permute-start(f32[1,230,256]{2,1,0:T(8,128)S(1)} %pad_maximum_fusion.2), channel_id=1, source_target_pairs={{0,8},{8,16},{16,24},{1,9},{9,17},{17,25},{2,10},{10,18},{18,26},{... | collective-permute-start | bytes 706568 | tf_op jit(solution)/shard_map/while/body/eval_jaxpr/ppermute | solution.py:14
  528.2 5.9 dynamic_update_slice.31
  544.5 24.5 %all_gather.15 = f32[1,20,2048]{2,1,0:T(8,128)S(1)} all-gather(f32[1,20,256]{2,1,0:T(8,128)S(1)} %slice.5342), channel_id=1, replica_groups=mesh['section'=4,'obs'=8] {'obs'}, dimensions={2}, use_global_device_ids=true | all-gather | bytes 184320 | tf_op jit(solution)/shard_map/while/body/eval_jaxpr/all_gather | solution.py:144
  586.9 4.3 all-to-all-start
  603.1 12.4 %collective-permute-start.3 = (f32[1,230,256]{2,1,0:T(8,128)S(1)}, f32[1,230,256]{2,1,0:T(8,128)S(1)}, u32[]{:S(2)}, u32[]{:S(2)}) collective-permute-start(f32[1,230,256]{2,1,0:T(8,128)S(1)} %pad_maximum_fusion.2), channel_id=1, source_target_pairs={{0,8},{8,16},{16,24},{1,9},{9,17},{17,25},{2,10},{10,18},{18,26},{... | collective-permute-start | bytes 706568 | tf_op jit(solution)/shard_map/while/body/eval_jaxpr/ppermute | solution.py:14
  615.9 5.9 dynamic_update_slice.31
  (704 shorter events, 248.9 us)
Async XLA Ops:
  7.5 50.8 %all-to-all-start.1 = ((f32[1,8,8]{2,0,1:T(1,128)}), f32[1,8,8]{2,0,1:T(1,128)S(1)}, u32[]{:S(2)}, u32[]{:S(2)}) async-start(f32[1,8,8]{2,0,1:T(1,128)} %bitcast.2462), calls=%async_computation.1 | async-start | bytes 8192 | tf_op jit(solution)/shard_map/while/body/eval_jaxpr/all_to_all | solution.py:162
  46.0 4.0 collective-permute-start
  55.0 3.3 collective-permute-start.2
  58.3 10.0 %all-to-all-start = ((f32[1,8,8,230]{3,2,0,1:T(8,128)}), f32[1,8,8,230]{3,2,0,1:T(8,128)S(1)}, u32[]{:S(2)}, u32[]{:S(2)}) async-start(f32[1,8,8,230]{3,2,0,1:T(8,128)} %convolution_bitcast_fusion.4), calls=%async_computation | async-start | bytes 131072 | tf_op jit(solution)/shard_map/while/body/eval_jaxpr/all_to_all | solution.py:161
  74.5 21.2 %collective-permute-start.3 = (f32[1,230,256]{2,1,0:T(8,128)S(1)}, f32[1,230,256]{2,1,0:T(8,128)S(1)}, u32[]{:S(2)}, u32[]{:S(2)}) collective-permute-start(f32[1,230,256]{2,1,0:T(8,128)S(1)} %pad_maximum_fusion.2), channel_id=1, source_target_pairs={{0,8},{8,16},{16,24},{1,9},{9,17},{17,25},{2,10},{10,18},{18,26},{... | collective-permute-start | bytes 706568 | tf_op jit(solution)/shard_map/while/body/eval_jaxpr/ppermute | solution.py:14
  100.3 48.0 %all-to-all-start.1 = ((f32[1,8,8]{2,0,1:T(1,128)}), f32[1,8,8]{2,0,1:T(1,128)S(1)}, u32[]{:S(2)}, u32[]{:S(2)}) async-start(f32[1,8,8]{2,0,1:T(1,128)} %bitcast.2462), calls=%async_computation.1 | async-start | bytes 8192 | tf_op jit(solution)/shard_map/while/body/eval_jaxpr/all_to_all | solution.py:162
  136.4 3.6 collective-permute-start
  148.4 10.0 %all-to-all-start = ((f32[1,8,8,230]{3,2,0,1:T(8,128)}), f32[1,8,8,230]{3,2,0,1:T(8,128)S(1)}, u32[]{:S(2)}, u32[]{:S(2)}) async-start(f32[1,8,8,230]{3,2,0,1:T(8,128)} %convolution_bitcast_fusion.4), calls=%async_computation | async-start | bytes 131072 | tf_op jit(solution)/shard_map/while/body/eval_jaxpr/all_to_all | solution.py:161
  164.6 18.8 %collective-permute-start.3 = (f32[1,230,256]{2,1,0:T(8,128)S(1)}, f32[1,230,256]{2,1,0:T(8,128)S(1)}, u32[]{:S(2)}, u32[]{:S(2)}) collective-permute-start(f32[1,230,256]{2,1,0:T(8,128)S(1)} %pad_maximum_fusion.2), channel_id=1, source_target_pairs={{0,8},{8,16},{16,24},{1,9},{9,17},{17,25},{2,10},{10,18},{18,26},{... | collective-permute-start | bytes 706568 | tf_op jit(solution)/shard_map/while/body/eval_jaxpr/ppermute | solution.py:14
  188.0 48.0 %all-to-all-start.1 = ((f32[1,8,8]{2,0,1:T(1,128)}), f32[1,8,8]{2,0,1:T(1,128)S(1)}, u32[]{:S(2)}, u32[]{:S(2)}) async-start(f32[1,8,8]{2,0,1:T(1,128)} %bitcast.2462), calls=%async_computation.1 | async-start | bytes 8192 | tf_op jit(solution)/shard_map/while/body/eval_jaxpr/all_to_all | solution.py:162
  223.6 4.0 collective-permute-start
  232.7 3.3 collective-permute-start.2
  236.0 10.0 %all-to-all-start = ((f32[1,8,8,230]{3,2,0,1:T(8,128)}), f32[1,8,8,230]{3,2,0,1:T(8,128)S(1)}, u32[]{:S(2)}, u32[]{:S(2)}) async-start(f32[1,8,8,230]{3,2,0,1:T(8,128)} %convolution_bitcast_fusion.4), calls=%async_computation | async-start | bytes 131072 | tf_op jit(solution)/shard_map/while/body/eval_jaxpr/all_to_all | solution.py:161
  252.2 18.9 %collective-permute-start.3 = (f32[1,230,256]{2,1,0:T(8,128)S(1)}, f32[1,230,256]{2,1,0:T(8,128)S(1)}, u32[]{:S(2)}, u32[]{:S(2)}) collective-permute-start(f32[1,230,256]{2,1,0:T(8,128)S(1)} %pad_maximum_fusion.2), channel_id=1, source_target_pairs={{0,8},{8,16},{16,24},{1,9},{9,17},{17,25},{2,10},{10,18},{18,26},{... | collective-permute-start | bytes 706568 | tf_op jit(solution)/shard_map/while/body/eval_jaxpr/ppermute | solution.py:14
  275.7 48.2 %all-to-all-start.1 = ((f32[1,8,8]{2,0,1:T(1,128)}), f32[1,8,8]{2,0,1:T(1,128)S(1)}, u32[]{:S(2)}, u32[]{:S(2)}) async-start(f32[1,8,8]{2,0,1:T(1,128)} %bitcast.2462), calls=%async_computation.1 | async-start | bytes 8192 | tf_op jit(solution)/shard_map/while/body/eval_jaxpr/all_to_all | solution.py:162
  311.4 4.2 collective-permute-start
  320.6 3.3 collective-permute-start.2
  323.9 10.0 %all-to-all-start = ((f32[1,8,8,230]{3,2,0,1:T(8,128)}), f32[1,8,8,230]{3,2,0,1:T(8,128)S(1)}, u32[]{:S(2)}, u32[]{:S(2)}) async-start(f32[1,8,8,230]{3,2,0,1:T(8,128)} %convolution_bitcast_fusion.4), calls=%async_computation | async-start | bytes 131072 | tf_op jit(solution)/shard_map/while/body/eval_jaxpr/all_to_all | solution.py:161
  340.1 18.7 %collective-permute-start.3 = (f32[1,230,256]{2,1,0:T(8,128)S(1)}, f32[1,230,256]{2,1,0:T(8,128)S(1)}, u32[]{:S(2)}, u32[]{:S(2)}) collective-permute-start(f32[1,230,256]{2,1,0:T(8,128)S(1)} %pad_maximum_fusion.2), channel_id=1, source_target_pairs={{0,8},{8,16},{16,24},{1,9},{9,17},{17,25},{2,10},{10,18},{18,26},{... | collective-permute-start | bytes 706568 | tf_op jit(solution)/shard_map/while/body/eval_jaxpr/ppermute | solution.py:14
  363.4 48.2 %all-to-all-start.1 = ((f32[1,8,8]{2,0,1:T(1,128)}), f32[1,8,8]{2,0,1:T(1,128)S(1)}, u32[]{:S(2)}, u32[]{:S(2)}) async-start(f32[1,8,8]{2,0,1:T(1,128)} %bitcast.2462), calls=%async_computation.1 | async-start | bytes 8192 | tf_op jit(solution)/shard_map/while/body/eval_jaxpr/all_to_all | solution.py:162
  399.2 4.0 collective-permute-start
  411.6 9.7 %all-to-all-start = ((f32[1,8,8,230]{3,2,0,1:T(8,128)}), f32[1,8,8,230]{3,2,0,1:T(8,128)S(1)}, u32[]{:S(2)}, u32[]{:S(2)}) async-start(f32[1,8,8,230]{3,2,0,1:T(8,128)} %convolution_bitcast_fusion.4), calls=%async_computation | async-start | bytes 131072 | tf_op jit(solution)/shard_map/while/body/eval_jaxpr/all_to_all | solution.py:161
  427.5 19.0 %collective-permute-start.3 = (f32[1,230,256]{2,1,0:T(8,128)S(1)}, f32[1,230,256]{2,1,0:T(8,128)S(1)}, u32[]{:S(2)}, u32[]{:S(2)}) collective-permute-start(f32[1,230,256]{2,1,0:T(8,128)S(1)} %pad_maximum_fusion.2), channel_id=1, source_target_pairs={{0,8},{8,16},{16,24},{1,9},{9,17},{17,25},{2,10},{10,18},{18,26},{... | collective-permute-start | bytes 706568 | tf_op jit(solution)/shard_map/while/body/eval_jaxpr/ppermute | solution.py:14
  451.1 48.1 %all-to-all-start.1 = ((f32[1,8,8]{2,0,1:T(1,128)}), f32[1,8,8]{2,0,1:T(1,128)S(1)}, u32[]{:S(2)}, u32[]{:S(2)}) async-start(f32[1,8,8]{2,0,1:T(1,128)} %bitcast.2462), calls=%async_computation.1 | async-start | bytes 8192 | tf_op jit(solution)/shard_map/while/body/eval_jaxpr/all_to_all | solution.py:162
  486.7 4.1 collective-permute-start
  495.8 3.3 collective-permute-start.2
  499.1 10.0 %all-to-all-start = ((f32[1,8,8,230]{3,2,0,1:T(8,128)}), f32[1,8,8,230]{3,2,0,1:T(8,128)S(1)}, u32[]{:S(2)}, u32[]{:S(2)}) async-start(f32[1,8,8,230]{3,2,0,1:T(8,128)} %convolution_bitcast_fusion.4), calls=%async_computation | async-start | bytes 131072 | tf_op jit(solution)/shard_map/while/body/eval_jaxpr/all_to_all | solution.py:161
  515.3 18.8 %collective-permute-start.3 = (f32[1,230,256]{2,1,0:T(8,128)S(1)}, f32[1,230,256]{2,1,0:T(8,128)S(1)}, u32[]{:S(2)}, u32[]{:S(2)}) collective-permute-start(f32[1,230,256]{2,1,0:T(8,128)S(1)} %pad_maximum_fusion.2), channel_id=1, source_target_pairs={{0,8},{8,16},{16,24},{1,9},{9,17},{17,25},{2,10},{10,18},{18,26},{... | collective-permute-start | bytes 706568 | tf_op jit(solution)/shard_map/while/body/eval_jaxpr/ppermute | solution.py:14
  538.7 48.2 %all-to-all-start.1 = ((f32[1,8,8]{2,0,1:T(1,128)}), f32[1,8,8]{2,0,1:T(1,128)S(1)}, u32[]{:S(2)}, u32[]{:S(2)}) async-start(f32[1,8,8]{2,0,1:T(1,128)} %bitcast.2462), calls=%async_computation.1 | async-start | bytes 8192 | tf_op jit(solution)/shard_map/while/body/eval_jaxpr/all_to_all | solution.py:162
  574.0 4.5 collective-permute-start
  586.9 10.0 %all-to-all-start = ((f32[1,8,8,230]{3,2,0,1:T(8,128)}), f32[1,8,8,230]{3,2,0,1:T(8,128)S(1)}, u32[]{:S(2)}, u32[]{:S(2)}) async-start(f32[1,8,8,230]{3,2,0,1:T(8,128)} %convolution_bitcast_fusion.4), calls=%async_computation | async-start | bytes 131072 | tf_op jit(solution)/shard_map/while/body/eval_jaxpr/all_to_all | solution.py:161
  603.1 18.7 %collective-permute-start.3 = (f32[1,230,256]{2,1,0:T(8,128)S(1)}, f32[1,230,256]{2,1,0:T(8,128)S(1)}, u32[]{:S(2)}, u32[]{:S(2)}) collective-permute-start(f32[1,230,256]{2,1,0:T(8,128)S(1)} %pad_maximum_fusion.2), channel_id=1, source_target_pairs={{0,8},{8,16},{16,24},{1,9},{9,17},{17,25},{2,10},{10,18},{18,26},{... | collective-permute-start | bytes 706568 | tf_op jit(solution)/shard_map/while/body/eval_jaxpr/ppermute | solution.py:14
  (36 other events, 44.9 us)
